TPU v7x, 32 devices: a whole 2x2x4 slice. The times are simulated.
32 devices in a mesh: enc: 4 (over y, x), dec: 4 (over z), ret: 2 (over core).
Axes of the slice: x: 2, y: 2, z: 4, core: 2. Of those that a mesh axis runs over, the one named last changes fastest.
Arguments:
- enc_states: bfloat16 [8, 2, 256, 4096], P('enc', 'ret'), may hold values from -22 to 22
- kv_weight: bfloat16 [4096, 64, 128], P(None, 'dec'), may hold values from -1 to 1
- queries: bfloat16 [2, 128, 64, 64], P('ret', None, ('dec', 'enc')), may hold values from -47 to 47
- out_grad: bfloat16 [2, 128, 64, 64], P('ret', None, ('dec', 'enc')), may hold values from -6 to 6
- passage_order: int32 [2, 8], P('ret'), may hold values from 0 to 7, each once within a row
- passage_blocks: int32 [2, 8], P('ret'), may hold values from 1 to 2
- ret_tokens: bfloat16 [8, 2, 256, 768], P('enc', 'ret'), may hold values from -6 to 6
- ret_weight: bfloat16 [768, 768], replicated, may hold values from -0.21875 to 0.21875
- question_emb: float32 [2, 768], P('ret'), may hold values from -7 to 7
Outputs:
- kv_grad: bfloat16 [8, 2, 256, 64, 128], P('enc', 'ret', None, 'dec')
- kv_weight_grad: bfloat16 [4096, 64, 128], P(('enc', 'ret'), 'dec')
- ret_weight_grad: bfloat16 [768, 768], replicated
Inputs may be any that keep to these rules, and one draw needn't show every extreme that they name: `passage_order`: each row lists every passage of its group once; slots i * 8 to (i + 1) * 8 - 1 belong to question i of the group.
All inputs are finite; a program needn't handle non-finite values.
Results may differ from a plain program's by a relative error of at most 0.025.
Values may be sent and summed in bfloat16 or wider, within the bound.
A program may use at most 128 MiB of HBM per device.

v0:
```python
import math
import jax
import jax.numpy as jnp
from jax import lax
from jax.sharding import PartitionSpec as P

HEADS = 64
BLK = 128
PASS = 8


def gelu_grad(pre_act, upstream):
    return jax.vjp(jax.nn.gelu, pre_act)[1](upstream)[0]


def on_device(
    enc_states,
    kv_weight,
    queries,
    out_grad,
    passage_order,
    passage_blocks,
    ret_tokens,
    ret_weight,
    question_emb,
):
    pass_dev = enc_states.shape[0]
    slot_len = enc_states.shape[2]
    width = enc_states.shape[3]
    heads_dec = kv_weight.shape[1]
    pair_width = kv_weight.shape[2]
    head_dim = pair_width // 2
    enc_rank = lax.axis_index("enc")
    dec_rank = lax.axis_index("dec")
    order_row = passage_order[0]
    blocks_row = passage_blocks[0]
    group_pass = order_row.shape[0]
    question_count = queries.shape[0]
    query_len = queries.shape[1]
    highest = lax.Precision.HIGHEST
    own_blocks = lax.dynamic_slice_in_dim(blocks_row, enc_rank * pass_dev, pass_dev)
    tok_rows = enc_states.reshape(pass_dev * slot_len, width)
    weight_flat = kv_weight.reshape(width, heads_dec * pair_width)
    key_value = jnp.dot(tok_rows, weight_flat, preferred_element_type=jnp.float32)
    key_value = key_value.reshape(pass_dev * slot_len, heads_dec, pair_width)
    gathered = lax.all_to_all(key_value, "enc", split_axis=1, concat_axis=0, tiled=True)
    heads_here = gathered.shape[1]
    gathered = gathered.reshape(group_pass, slot_len, heads_here, pair_width)
    chosen = order_row.reshape(question_count, PASS)
    key_count = PASS * slot_len
    selected = gathered[chosen].reshape(question_count, key_count, heads_here, pair_width)
    keys = selected[..., :head_dim]
    values = selected[..., head_dim:]
    positions = jnp.arange(slot_len, dtype=jnp.int32)
    live = (positions[None, None, :] < BLK * blocks_row[chosen][:, :, None]).reshape(
        question_count, key_count
    )
    scale = 1.0 / math.sqrt(head_dim)
    query_wide = queries.astype(jnp.float32)
    grad_wide = out_grad.astype(jnp.float32)
    scores = jnp.einsum("qlhc,qkhc->qhlk", query_wide, keys, precision=highest) * scale
    masked = jnp.where(live[:, None, None, :], scores, -1e30)
    top = jnp.max(masked, axis=-1, keepdims=True)
    expo = jnp.where(live[:, None, None, :], jnp.exp(masked - top), 0.0)
    probs = expo / jnp.sum(expo, axis=-1, keepdims=True)
    probs_low = probs.astype(jnp.bfloat16)
    attended = jnp.einsum(
        "qhlk,qkhc->qlhc", probs_low.astype(jnp.float32), values, precision=highest
    )
    value_grad = jnp.einsum(
        "qhlk,qlhc->qkhc", probs_low, out_grad, preferred_element_type=jnp.float32
    )
    prob_grad = jnp.einsum("qlhc,qkhc->qhlk", grad_wide, values, precision=highest)
    row_dot = jnp.einsum("qlhc,qlhc->qhl", grad_wide, attended)
    score_grad = (probs * (prob_grad - row_dot[..., None]) * scale).astype(jnp.bfloat16)
    key_grad = jnp.einsum(
        "qhlk,qlhc->qkhc", score_grad, queries, preferred_element_type=jnp.float32
    )
    pair_grad = jnp.concatenate([key_grad, value_grad], axis=-1).astype(jnp.bfloat16)
    pair_grad = pair_grad.reshape(question_count * PASS, slot_len, heads_here, pair_width)
    placed = (
        jnp.zeros((group_pass, slot_len, heads_here, pair_width), jnp.bfloat16)
        .at[order_row]
        .set(pair_grad)
    )
    returned = lax.all_to_all(
        placed.reshape(group_pass * slot_len, heads_here, pair_width),
        "enc",
        split_axis=0,
        concat_axis=1,
        tiled=True,
    )
    kv_grad = returned.reshape(pass_dev, 1, slot_len, heads_dec, pair_width)
    mass_part = jnp.sum(probs, axis=(1, 2)).reshape(question_count, PASS, slot_len).sum(axis=-1) / (
        HEADS * query_len
    )
    ret_rows = ret_tokens.reshape(pass_dev * slot_len, ret_tokens.shape[3])
    ret_width = ret_rows.shape[1]
    pre_act = jnp.dot(ret_rows, ret_weight, preferred_element_type=jnp.float32).reshape(
        pass_dev, slot_len, ret_width
    )
    hidden = jax.nn.gelu(pre_act)
    own_live = positions[None, :] < BLK * own_blocks[:, None]
    own_length = (BLK * own_blocks).astype(jnp.float32)
    embed_own = jnp.sum(jnp.where(own_live[..., None], hidden, 0.0), axis=1) / own_length[:, None]
    owner_map = (
        order_row[:, None] == enc_rank * pass_dev + jnp.arange(pass_dev, dtype=jnp.int32)[None, :]
    ).astype(jnp.float32)
    slot_embed = jnp.dot(owner_map, embed_own, precision=highest)
    emb_rep = jnp.repeat(question_emb, PASS, axis=0)
    score_part = jnp.sum(emb_rep * slot_embed, axis=-1) * (dec_rank == 0).astype(jnp.float32)
    passage_mass, ret_scores = lax.psum(
        (mass_part, score_part.reshape(question_count, PASS)), ("enc", "dec")
    )
    top_score = jnp.max(ret_scores, axis=-1, keepdims=True)
    expo_score = jnp.exp(ret_scores - top_score)
    score_gap = expo_score / jnp.sum(expo_score, axis=-1, keepdims=True) - passage_mass
    gap_rows = score_gap.reshape(-1, 1) * emb_rep
    embed_grad = jnp.dot(jnp.transpose(owner_map), gap_rows, precision=highest)
    hidden_grad = jnp.where(
        own_live[..., None], (embed_grad / own_length[:, None])[:, None, :], 0.0
    )
    pre_grad = gelu_grad(pre_act, hidden_grad).astype(jnp.bfloat16)
    ret_part_grad = lax.dot_general(
        ret_rows,
        pre_grad.reshape(-1, ret_width),
        (((0,), (0,)), ((), ())),
        preferred_element_type=jnp.float32,
    )
    ret_weight_grad = lax.psum(ret_part_grad.astype(jnp.bfloat16), ("enc", "ret"))
    grad_flat = returned.reshape(pass_dev * slot_len, heads_dec * pair_width)
    term = lax.dot_general(
        tok_rows, grad_flat, (((0,), (0,)), ((), ())), preferred_element_type=jnp.float32
    )
    weight_total = lax.psum_scatter(
        term.reshape(
            width // (lax.axis_size("enc") * lax.axis_size("ret")) * lax.axis_size(("enc", "ret")),
            heads_dec,
            pair_width,
        ).astype(jnp.bfloat16),
        ("enc", "ret"),
        scatter_dimension=0,
        tiled=True,
    )
    return (kv_grad, weight_total, ret_weight_grad)


def solution(mesh):
    return jax.shard_map(
        on_device,
        mesh=mesh,
        in_specs=(
            P("enc", "ret", None, None),
            P(None, "dec", None),
            P("ret", None, ("dec", "enc"), None),
            P("ret", None, ("dec", "enc"), None),
            P("ret", None),
            P("ret", None),
            P("enc", "ret", None, None),
            P(),
            P("ret", None),
        ),
        out_specs=(P("enc", "ret", None, "dec", None), P(("enc", "ret"), "dec", None), P()),
        check_vma=False,
    )
```

profile of v0, /device:TPU:0, one launch (start us, length us, event | category | flops | bytes accessed | tf_op | source)
XLA Modules:
  0.0 412.8 jit_solution(12834699166763895516)
XLA Ops:
  7.2 17.3 %copy.95 = bf16[512,8,16,128]{3,1,2,0:T(8,128)(2,1)} copy(bf16[512,8,16,128]{3,2,1,0:T(8,128)(2,1)} %bitcast.155) | data formatting | bytes 33554432
  24.5 20.7 %copy.64 = bf16[2048,4096]{1,0:T(8,128)(2,1)} copy(bf16[2048,4096]{0,1:T(8,128)(2,1)} %bitcast.152) | data formatting | bytes 33554432 | tf_op jit(solution)/shard_map/dot_general | solution.py:44
  45.3 14.2 %fusion.57 = f32[512,16,128]{2,0,1:T(8,128)} fusion(bf16[512,4096,1]{1,0,2:T(8,128)(2,1)} %bitcast.169, bf16[16,128,4096]{2,1,0:T(8,128)(2,1)} %bitcast.156), kind=kOutput, calls=%fused_computation.90 | convolution fusion | flops 8589934592 | bytes 25165824 | tf_op jit(solution)/shard_map/dot_general | solution.py:44
  59.4 5.3 %all-to-all-start = ((f32[512,16,128]{2,0,1:T(8,128)}), f32[512,16,128]{2,0,1:T(8,128)}, u32[]{:S(2)}, u32[]{:S(2)}) async-start(f32[512,16,128]{2,0,1:T(8,128)} %fusion.57), calls=%async_computation | async-start | bytes 8388608 | tf_op jit(solution)/shard_map/all_to_all | solution.py:46
  68.3 45.3 %all-to-all-done = f32[512,16,128]{2,0,1:T(8,128)} async-done(((f32[512,16,128]{2,0,1:T(8,128)}), f32[512,16,128]{2,0,1:T(8,128)}, u32[]{:S(2)}, u32[]{:S(2)}) %all-to-all-start) | async-done | bytes 4194336 | tf_op jit(solution)/shard_map/all_to_all | solution.py:46
  113.6 2.5 copy.65
  118.3 4.9 %gather_fusion.1 = f32[8,256,4,128]{3,1,2,0:T(8,128)} fusion(f32[8,256,4,128]{3,1,2,0:T(8,128)} %copy.66, s32[1024]{0:T(1024)S(1)} %pad_clamp_fusion), kind=kCustom, calls=%fused_computation.1 | custom fusion | bytes 8388640 | tf_op jit(solution)/shard_map/gather | solution.py:51
  123.3 5.4 %copy.67 = f32[8,256,4,128]{1,0,3,2:T(8,128)} copy(f32[8,256,4,128]{3,1,2,0:T(8,128)} %gather_fusion.1) | data formatting | bytes 8388608 | tf_op jit(solution)/shard_map/gather | solution.py:51
  128.7 4.9 %reshape.262 = f32[1,2048,4,128]{1,3,2,0:T(8,128)} reshape(f32[8,256,4,128]{1,0,3,2:T(8,128)} %copy.67) | data formatting | bytes 8388608 | tf_op jit(solution)/shard_map/reshape | solution.py:51
  133.6 5.1 %fusion.8 = f32[4,2048,128]{2,1,0:T(8,128)S(1)} fusion(f32[1,2048,4,128]{1,3,2,0:T(8,128)} %reshape.262, bf16[1,128,4,64]{1,3,2,0:T(8,128)(2,1)S(1)} %copy-done.6), kind=kOutput, calls=%fused_computation.23 | convolution fusion | flops 805306368 | bytes 6356992 | tf_op jit(solution)/shard_map/qlhc,qkhc->qhlk/dot_general | solution.py:61
  144.1 4.0 fusion.2
  155.9 4.1 pad_maximum_fusion
  160.5 3.3 scatter_fusion
  164.0 10.7 %copy.74 = bf16[2048,4,128]{2,1,0:T(4,128)(2,1)} copy(bf16[2048,4,128]{2,0,1:T(8,128)(2,1)S(1)} %bitcast.159) | data formatting | bytes 4194304 | tf_op jit(solution)/shard_map/reshape | solution.py:87
  174.7 4.4 %all-to-all-start.1 = ((bf16[2048,4,128]{2,1,0:T(4,128)(2,1)}), bf16[2048,4,128]{2,1,0:T(4,128)(2,1)}, u32[]{:S(2)}, u32[]{:S(2)}) async-start(bf16[2048,4,128]{2,1,0:T(4,128)(2,1)} %copy.74), calls=%async_computation.1 | async-start | bytes 4194304 | tf_op jit(solution)/shard_map/all_to_all | solution.py:86
  179.2 2.7 fusion.54
  182.0 42.9 %all-reduce = (f32[1,8]{1,0:T(1,128)S(1)}, f32[1,8]{1,0:T(1,128)S(1)}) all-reduce(f32[1,8]{1,0:T(1,128)S(1)} %get-tuple-element.26, f32[1,8]{1,0:T(1,128)S(1)} %get-tuple-element.27), channel_id=1, replica_groups=mesh['enc'=4,'dec'=4,'ret'=2] {'enc','dec'}, use_global_device_ids=true, to_apply=%region_11.12 | all-reduce | flops 16 | bytes 128 | tf_op jit(solution)/shard_map/psum | solution.py:112
  229.5 3.0 fusion.23
  237.0 14.8 %convolution_convert_fusion = bf16[2048,4096]{1,0:T(8,128)(2,1)} fusion(bf16[512,2048]{0,1:T(8,128)(2,1)} %bitcast.164, bf16[512,4096]{1,0:T(8,128)(2,1)} %bitcast.170), kind=kOutput, calls=%fused_computation.5 | convolution fusion | flops 8598323200 | bytes 23068672 | tf_op jit(solution)/shard_map/dot_general | solution.py:132
  251.8 22.3 %copy.78 = bf16[4096,16,128]{2,1,0:T(8,128)(2,1)} copy(bf16[4096,16,128]{0,2,1:T(8,128)(2,1)} %bitcast.157) | data formatting | bytes 33554432 | tf_op jit(solution)/shard_map/convert_element_type | solution.py:140
  274.2 12.1 %all-reduce.3.cloned.1.call-done = bf16[768,768]{0,1:T(8,128)(2,1)} async-done(((bf16[768,768]{0,1:T(8,128)(2,1)}), bf16[768,768]{0,1:T(8,128)(2,1)}) %all-reduce.3.cloned.1.call-update) | async-done | bytes 1179664 | tf_op jit(solution)/shard_map/psum | solution.py:130
  286.3 2.4 copy.80
  288.9 2.7 copy.79
  291.5 114.4 %reduce-scatter.2.cloned.1.call-done = bf16[512,16,128]{2,1,0:T(8,128)(2,1)} async-done(((bf16[4096,16,128]{2,1,0:T(8,128)(2,1)}), bf16[512,16,128]{2,1,0:T(8,128)(2,1)}) %reduce-scatter.2.cloned.1.call-update) | async-done | bytes 2097168 | tf_op jit(solution)/shard_map/reduce_scatter | solution.py:135
  (64 shorter events, 29.0 us)
Async XLA Ops:
  7.2 58.6 %copy-start = (bf16[768,768]{1,0:T(8,128)(2,1)S(1)}, bf16[768,768]{1,0:T(8,128)(2,1)}, u32[]{:S(2)}) copy-start(bf16[768,768]{1,0:T(8,128)(2,1)} %param.16) | copy-start | bytes 3538948
  59.4 5.4 %copy-start.7 = (f32[1,768]{1,0:T(1,128)S(1)}, f32[1,768]{1,0:T(1,128)}, u32[]{:S(2)}) copy-start(f32[1,768]{1,0:T(1,128)} %param.17) | copy-start | bytes 9220
  59.4 5.4 %copy-start.10 = (s32[1,8]{1,0:T(1,128)S(1)}, s32[1,8]{1,0:T(1,128)}, u32[]{:S(2)}) copy-start(s32[1,8]{1,0:T(1,128)} %param.13) | copy-start | bytes 100
  59.4 5.4 %copy-start.2 = (s32[1,8]{1,0:T(1,128)S(1)}, s32[1,8]{1,0:T(1,128)}, u32[]{:S(2)}) copy-start(s32[1,8]{1,0:T(1,128)} %param.14) | copy-start | bytes 100
  59.4 6.4 %copy-start.8 = (bf16[2,1,256,768]{3,2,1,0:T(8,128)(2,1)S(1)}, bf16[2,1,256,768]{3,2,1,0:T(8,128)(2,1)}, u32[]{:S(2)}) copy-start(bf16[2,1,256,768]{3,2,1,0:T(8,128)(2,1)} %param.15) | copy-start | bytes 2359300
  59.4 54.1 %all-to-all-start = ((f32[512,16,128]{2,0,1:T(8,128)}), f32[512,16,128]{2,0,1:T(8,128)}, u32[]{:S(2)}, u32[]{:S(2)}) async-start(f32[512,16,128]{2,0,1:T(8,128)} %fusion.57), calls=%async_computation | async-start | bytes 8388608 | tf_op jit(solution)/shard_map/all_to_all | solution.py:46
  128.7 4.9 %copy-start.6 = (bf16[1,128,4,64]{1,3,2,0:T(8,128)(2,1)S(1)}, bf16[1,128,4,64]{1,3,2,0:T(8,128)(2,1)}, u32[]{:S(2)}) copy-start(bf16[1,128,4,64]{1,3,2,0:T(8,128)(2,1)} %param.11) | copy-start | bytes 196612
  138.7 2.2 copy-start.3
  138.7 2.2 copy-start.9
  140.3 3.8 copy-start.4
  174.7 58.1 %all-to-all-start.1 = ((bf16[2048,4,128]{2,1,0:T(4,128)(2,1)}), bf16[2048,4,128]{2,1,0:T(4,128)(2,1)}, u32[]{:S(2)}, u32[]{:S(2)}) async-start(bf16[2048,4,128]{2,1,0:T(4,128)(2,1)} %copy.74), calls=%async_computation.1 | async-start | bytes 4194304 | tf_op jit(solution)/shard_map/all_to_all | solution.py:86
  179.1 49.2 %copy-start.5 = (f32[2,256,768]{2,1,0:T(8,128)S(1)}, f32[2,256,768]{2,1,0:T(8,128)}, u32[]{:S(2)}) copy-start(f32[2,256,768]{2,1,0:T(8,128)} %get-tuple-element.25) | copy-start | bytes 4718596
  179.1 107.2 %all-reduce.3.cloned.1.call-start = ((), (), s32[]{:S(2)}) async-start(), calls=%async_computation.4 | async-start | bytes 2359296 | tf_op jit(solution)/shard_map/psum | solution.py:130
  232.5 173.5 %reduce-scatter.2.cloned.1.call-start = ((), (), s32[]{:S(2)}) async-start(), calls=%async_computation.3 | async-start | bytes 18874368 | tf_op jit(solution)/shard_map/reduce_scatter | solution.py:135
  288.9 117.1 %copy-start.1 = (bf16[768,768]{1,0:T(8,128)(2,1)S(1)}, bf16[768,768]{1,0:T(8,128)(2,1)}, u32[]{:S(2)}) copy-start(bf16[768,768]{1,0:T(8,128)(2,1)} %param.16) | copy-start | bytes 3538948
Sparse Core Ops, SparseCore 0:
  232.6 53.6 all-reduce.2
  290.5 115.4 reduce-scatter.1
where the time goes:
time: 415 us; the launch traced here: 413 us
  waiting for transfers between devices  172 us (41%)
  local copies, waits for them, and re-layouts  113 us (27%)
  matrix products  47.9 us (12%)
  blocking collectives  42.9 us (10%)
  between operations  14.3 us (3%)
  other arithmetic  12.9 us (3%)
  starting transfers between devices  10.1 us (2%)
    reduce_scatter x1, waiting for transfers between devices, on_device(): lax.psum_scatter(term.reshape(width // (lax.axis_size('enc') * lax.axis_s...  114 us
    all_to_all x1, waiting for transfers between devices, on_device(): lax.all_to_all(key_value, 'enc', split_axis=1, concat_axis=0, tiled=True)  45.3 us
    psum x1, blocking collectives, on_device(): lax.psum((mass_part, score_part.reshape(question_count, PASS)), ('enc', '...  42.9 us
    unnamed x29, local copies, waits for them, and re-layouts  25.9 us
    convert_element_type x1, local copies, waits for them, and re-layouts, on_device(): weight_total = lax.psum_scatter(term.reshape(width // (lax.axis_size('enc...  22.3 us
    dot_general x1, local copies, waits for them, and re-layouts, on_device(): jnp.dot(tok_rows, weight_flat, preferred_element_type=jnp.float32)  20.7 us
    dot_general x1, matrix products, on_device(): lax.dot_general(tok_rows, grad_flat, (((0,), (0,)), ((), ())), preferred_...  14.8 us
    dot_general x1, matrix products, on_device(): jnp.dot(tok_rows, weight_flat, preferred_element_type=jnp.float32)  14.2 us
  transfers between devices with their start and end apart: 4, of which 3 were waited for; matrix products, arithmetic and copies ran while one was open for 15% of the time, Pallas kernels for 0%

commit v1 on v0

--- a/solution.py
+++ b/solution.py
@@ -7,6 +7,18 @@
 HEADS = 64
 BLK = 128
 PASS = 8
+
+
+def split_up(array, dim, devices):
+    lengths = array.shape
+    blocks = array.reshape(*lengths[:dim], devices, lengths[dim] // devices, *lengths[dim + 1 :])
+    return jnp.moveaxis(blocks, dim, 0)
+
+
+def joined_along(blocks, dim):
+    lengths = list(blocks.shape[1:])
+    lengths[dim] *= blocks.shape[0]
+    return jnp.moveaxis(blocks, 0, dim).reshape(lengths)
 
 
 def gelu_grad(pre_act, upstream):
@@ -43,7 +55,16 @@
     weight_flat = kv_weight.reshape(width, heads_dec * pair_width)
     key_value = jnp.dot(tok_rows, weight_flat, preferred_element_type=jnp.float32)
     key_value = key_value.reshape(pass_dev * slot_len, heads_dec, pair_width)
-    gathered = lax.all_to_all(key_value, "enc", split_axis=1, concat_axis=0, tiled=True)
+    count, index = (lax.axis_size("enc"), lax.axis_index("enc"))
+    parts = split_up(key_value, 1, count)
+    gathered_2 = [parts[index]]
+    for step in range(1, count):
+        sent = parts[(index + step) % count]
+        gathered_2.append(
+            lax.ppermute(sent, "enc", [(i, (i + step) % count) for i in range(count)])
+        )
+    parts = jnp.stack(gathered_2)[(index - jnp.arange(count)) % count]
+    gathered = joined_along(parts, 0)
     heads_here = gathered.shape[1]
     gathered = gathered.reshape(group_pass, slot_len, heads_here, pair_width)
     chosen = order_row.reshape(question_count, PASS)

time: 415 us -> 419 us (level)
  local copies, waits for them, and re-layouts: 113 us -> 120 us
  waiting for transfers between devices: 172 us -> 166 us
  other arithmetic: 12.9 us -> 17.1 us
    all_to_all x1 -> x0, waiting for transfers between devices: 45.3 us -> none  [on_device(): lax.all_to_all(key_value, 'enc', split_axis=1, concat_axis=0, tiled=True)]
    ppermute x0 -> x3, waiting for transfers between devices: none -> 39.6 us  [on_device(): lax.ppermute(sent, 'enc', [(i, (i + step) % count) for i in range(count)])]
    gather x0 -> x2, local copies, waits for them, and re-layouts: none -> 7.45 us  [on_device(): parts = jnp.stack(gathered_2)[(index - jnp.arange(count)) % count]]
    ppermute x0 -> x3, starting transfers between devices: none -> 5.92 us  [on_device(): lax.ppermute(sent, 'enc', [(i, (i + step) % count) for i in range(count)])]
    all_to_all x1 -> x0, starting transfers between devices: 5.33 us -> none  [on_device(): lax.all_to_all(key_value, 'enc', split_axis=1, concat_axis=0, tiled=True)]
    unnamed x29 -> x27, local copies, waits for them, and re-layouts: 25.9 us -> 25.9 us
  transfers between devices with their start and end apart: 4 -> 6, of which waited for: 3 -> 5; matrix products, arithmetic and copies ran while one was open for 15% -> 15% of each run, Pallas kernels for 0% -> 0%
where the time goes in v1:
time: 419 us; the launch traced here: 417 us
  waiting for transfers between devices  166 us (40%)
  local copies, waits for them, and re-layouts  120 us (29%)
  matrix products  46.9 us (11%)
  blocking collectives  43 us (10%)
  other arithmetic  17.1 us (4%)
  between operations  14.4 us (3%)
  starting transfers between devices  10.4 us (2%)
    reduce_scatter x1, waiting for transfers between devices, on_device(): lax.psum_scatter(term.reshape(width // (lax.axis_size('enc') * lax.axis_s...  114 us
    psum x1, blocking collectives, on_device(): lax.psum((mass_part, score_part.reshape(question_count, PASS)), ('enc', '...  43 us
    ppermute x3, waiting for transfers between devices, on_device(): lax.ppermute(sent, 'enc', [(i, (i + step) % count) for i in range(count)])  39.6 us
    unnamed x27, local copies, waits for them, and re-layouts  25.9 us
    convert_element_type x1, local copies, waits for them, and re-layouts, on_device(): weight_total = lax.psum_scatter(term.reshape(width // (lax.axis_size('enc...  22.3 us
    dot_general x1, local copies, waits for them, and re-layouts, on_device(): jnp.dot(tok_rows, weight_flat, preferred_element_type=jnp.float32)  20.7 us
    dot_general x1, matrix products, on_device(): lax.dot_general(tok_rows, grad_flat, (((0,), (0,)), ((), ())), preferred_...  14.8 us
    dot_general x1, matrix products, on_device(): jnp.dot(tok_rows, weight_flat, preferred_element_type=jnp.float32)  12.3 us
  transfers between devices with their start and end apart: 6, of which 5 were waited for; matrix products, arithmetic and copies ran while one was open for 15% of the time, Pallas kernels for 0%

profile of v1, /device:TPU:0, one launch (start us, length us, event | category | flops | bytes accessed | tf_op | source)
XLA Modules:
  0.0 417.3 jit_solution(12259259670835769256)
XLA Ops:
  7.2 17.3 %copy.95 = bf16[512,8,16,128]{3,1,2,0:T(8,128)(2,1)} copy(bf16[512,8,16,128]{3,2,1,0:T(8,128)(2,1)} %bitcast.167) | data formatting | bytes 33554432
  24.6 20.7 %copy.63 = bf16[2048,4096]{1,0:T(8,128)(2,1)} copy(bf16[2048,4096]{0,1:T(8,128)(2,1)} %bitcast.164) | data formatting | bytes 33554432 | tf_op jit(solution)/shard_map/dot_general | solution.py:56
  45.3 12.3 %fusion.62 = f32[512,4,4,128]{3,0,2,1:T(8,128)S(1)} fusion(bf16[512,4096,1,1]{1,0,3,2:T(8,128)(2,1)} %bitcast.181, bf16[4,4,128,4096]{3,2,1,0:T(8,128)(2,1)} %bitcast.168), kind=kOutput, calls=%fused_computation.105 | convolution fusion | flops 8589934592 | bytes 25165824 | tf_op jit(solution)/shard_map/dot_general | solution.py:56
  59.3 3.0 collective-permute-start
  66.2 3.3 select_reduce_fusion
  69.9 17.7 %collective-permute-done = f32[512,4,128]{2,0,1:T(8,128)} collective-permute-done((f32[512,4,128]{2,0,1:T(8,128)}, f32[512,4,128]{2,0,1:T(8,128)}, u32[]{:S(2)}, u32[]{:S(2)}) %collective-permute-start) | collective-permute-done | bytes 1048608 | tf_op jit(solution)/shard_map/ppermute | solution.py:64
  87.5 21.6 %collective-permute-done.1 = f32[512,4,128]{2,0,1:T(8,128)} collective-permute-done((f32[512,4,128]{2,0,1:T(8,128)}, f32[512,4,128]{2,0,1:T(8,128)}, u32[]{:S(2)}, u32[]{:S(2)}) %collective-permute-start.1) | collective-permute-done | bytes 1048608 | tf_op jit(solution)/shard_map/ppermute | solution.py:64
  109.4 4.1 pad_maximum_fusion
  113.6 5.0 %gather_fusion.1 = f32[4,512,4,128]{3,1,2,0:T(8,128)} fusion(f32[4,512,4,128]{3,1,2,0:T(8,128)} %pad_maximum_fusion, s32[1024]{0:T(1024)S(1)} %pad_clamp_fusion), kind=kCustom, calls=%fused_computation.1 | custom fusion | bytes 8388624 | tf_op jit(solution)/shard_map/gather | solution.py:66
  123.3 4.9 %gather_fusion.2 = f32[8,256,4,128]{3,1,2,0:T(8,128)} fusion(f32[8,256,4,128]{3,1,2,0:T(8,128)} %copy.65, s32[1024]{0:T(1024)S(1)} %pad_clamp_fusion.1), kind=kCustom, calls=%fused_computation.2 | custom fusion | bytes 8388640 | tf_op jit(solution)/shard_map/gather | solution.py:72
  128.2 5.4 %copy.66 = f32[8,256,4,128]{1,0,3,2:T(8,128)} copy(f32[8,256,4,128]{3,1,2,0:T(8,128)} %gather_fusion.2) | data formatting | bytes 8388608 | tf_op jit(solution)/shard_map/gather | solution.py:72
  133.7 4.9 %reshape.312 = f32[1,2048,4,128]{1,3,2,0:T(8,128)} reshape(f32[8,256,4,128]{1,0,3,2:T(8,128)} %copy.66) | data formatting | bytes 8388608 | tf_op jit(solution)/shard_map/reshape | solution.py:72
  138.6 5.1 %fusion.8 = f32[4,2048,128]{2,1,0:T(8,128)S(1)} fusion(f32[1,2048,4,128]{1,3,2,0:T(8,128)} %reshape.312, bf16[1,128,4,64]{1,3,2,0:T(8,128)(2,1)S(1)} %copy-done.6), kind=kOutput, calls=%fused_computation.25 | convolution fusion | flops 805306368 | bytes 6356992 | tf_op jit(solution)/shard_map/qlhc,qkhc->qhlk/dot_general | solution.py:82
  149.0 3.8 fusion.2
  160.7 4.1 pad_maximum_fusion.1
  165.2 3.3 scatter_fusion
  168.7 10.7 %copy.73 = bf16[2048,4,128]{2,1,0:T(4,128)(2,1)} copy(bf16[2048,4,128]{2,0,1:T(8,128)(2,1)S(1)} %bitcast.171) | data formatting | bytes 4194304 | tf_op jit(solution)/shard_map/reshape | solution.py:108
  179.4 4.4 %all-to-all-start = ((bf16[2048,4,128]{2,1,0:T(4,128)(2,1)}), bf16[2048,4,128]{2,1,0:T(4,128)(2,1)}, u32[]{:S(2)}, u32[]{:S(2)}) async-start(bf16[2048,4,128]{2,1,0:T(4,128)(2,1)} %copy.73), calls=%async_computation | async-start | bytes 4194304 | tf_op jit(solution)/shard_map/all_to_all | solution.py:107
  186.7 43.0 %all-reduce = (f32[1,8]{1,0:T(1,128)S(1)}, f32[1,8]{1,0:T(1,128)S(1)}) all-reduce(f32[1,8]{1,0:T(1,128)S(1)} %get-tuple-element.30, f32[1,8]{1,0:T(1,128)S(1)} %get-tuple-element.31), channel_id=1, replica_groups=mesh['enc'=4,'dec'=4,'ret'=2] {'enc','dec'}, use_global_device_ids=true, to_apply=%region_11.12 | all-reduce | flops 16 | bytes 128 | tf_op jit(solution)/shard_map/psum | solution.py:133
  234.3 3.0 fusion.23
  241.8 14.8 %convolution_convert_fusion = bf16[2048,4096]{1,0:T(8,128)(2,1)} fusion(bf16[512,2048]{0,1:T(8,128)(2,1)} %bitcast.176, bf16[512,4096]{1,0:T(8,128)(2,1)} %bitcast.182), kind=kOutput, calls=%fused_computation.6 | convolution fusion | flops 8598323200 | bytes 23068672 | tf_op jit(solution)/shard_map/dot_general | solution.py:153
  256.6 22.3 %copy.77 = bf16[4096,16,128]{2,1,0:T(8,128)(2,1)} copy(bf16[4096,16,128]{0,2,1:T(8,128)(2,1)} %bitcast.169) | data formatting | bytes 33554432 | tf_op jit(solution)/shard_map/convert_element_type | solution.py:161
  279.0 11.8 %all-reduce.3.cloned.1.call-done = bf16[768,768]{0,1:T(8,128)(2,1)} async-done(((bf16[768,768]{0,1:T(8,128)(2,1)}), bf16[768,768]{0,1:T(8,128)(2,1)}) %all-reduce.3.cloned.1.call-update) | async-done | bytes 1179664 | tf_op jit(solution)/shard_map/psum | solution.py:151
  296.0 114.4 %reduce-scatter.2.cloned.1.call-done = bf16[512,16,128]{2,1,0:T(8,128)(2,1)} async-done(((bf16[4096,16,128]{2,1,0:T(8,128)(2,1)}), bf16[512,16,128]{2,1,0:T(8,128)(2,1)}) %reduce-scatter.2.cloned.1.call-update) | async-done | bytes 2097168 | tf_op jit(solution)/shard_map/reduce_scatter | solution.py:156
  (71 shorter events, 41.8 us)
Async XLA Ops:
  7.2 59.0 %copy-start = (bf16[768,768]{1,0:T(8,128)(2,1)S(1)}, bf16[768,768]{1,0:T(8,128)(2,1)}, u32[]{:S(2)}) copy-start(bf16[768,768]{1,0:T(8,128)(2,1)} %param.16) | copy-start | bytes 3538948
  57.6 7.6 %copy-start.9 = (s32[1,8]{1,0:T(1,128)S(1)}, s32[1,8]{1,0:T(1,128)}, u32[]{:S(2)}) copy-start(s32[1,8]{1,0:T(1,128)} %param.13) | copy-start | bytes 100
  57.6 7.6 %copy-start.2 = (s32[1,8]{1,0:T(1,128)S(1)}, s32[1,8]{1,0:T(1,128)}, u32[]{:S(2)}) copy-start(s32[1,8]{1,0:T(1,128)} %param.14) | copy-start | bytes 100
  57.6 8.5 %copy-start.7 = (f32[1,768]{1,0:T(1,128)S(1)}, f32[1,768]{1,0:T(1,128)}, u32[]{:S(2)}) copy-start(f32[1,768]{1,0:T(1,128)} %param.17) | copy-start | bytes 9220
  59.3 28.3 %collective-permute-start = (f32[512,4,128]{2,0,1:T(8,128)}, f32[512,4,128]{2,0,1:T(8,128)}, u32[]{:S(2)}, u32[]{:S(2)}) collective-permute-start(f32[512,4,128]{2,0,1:T(8,128)} %get-tuple-element.25), channel_id=1, source_target_pairs={{0,8},{8,16},{16,24},{24,0},{1,9},{9,17},{17,25},{25,1},{2,10},{10... | collective-permute-start | bytes 3145736 | tf_op jit(solution)/shard_map/ppermute | solution.py:64
  62.2 46.9 %collective-permute-start.1 = (f32[512,4,128]{2,0,1:T(8,128)}, f32[512,4,128]{2,0,1:T(8,128)}, u32[]{:S(2)}, u32[]{:S(2)}) collective-permute-start(f32[512,4,128]{2,0,1:T(8,128)} %get-tuple-element.24), channel_id=1, source_target_pairs={{0,16},{8,24},{16,0},{24,8},{1,17},{9,25},{17,1},{25,9},{2,18},{10... | collective-permute-start | bytes 3145736 | tf_op jit(solution)/shard_map/ppermute | solution.py:64
  63.7 45.7 %collective-permute-start.2 = (f32[512,4,128]{2,0,1:T(8,128)S(1)}, f32[512,4,128]{2,0,1:T(8,128)}, u32[]{:S(2)}, u32[]{:S(2)}) collective-permute-start(f32[512,4,128]{2,0,1:T(8,128)S(1)} %get-tuple-element.23), channel_id=1, source_target_pairs={{0,24},{8,0},{16,8},{24,16},{1,25},{9,1},{17,9},{25,17},{2,26},{10... | collective-permute-start | bytes 3145736 | tf_op jit(solution)/shard_map/ppermute | solution.py:64
  133.7 4.9 %copy-start.6 = (bf16[1,128,4,64]{1,3,2,0:T(8,128)(2,1)S(1)}, bf16[1,128,4,64]{1,3,2,0:T(8,128)(2,1)}, u32[]{:S(2)}) copy-start(bf16[1,128,4,64]{1,3,2,0:T(8,128)(2,1)} %param.11) | copy-start | bytes 196612
  143.6 2.2 copy-start.3
  143.6 2.2 copy-start.8
  145.2 3.8 copy-start.4
  179.4 57.9 %all-to-all-start = ((bf16[2048,4,128]{2,1,0:T(4,128)(2,1)}), bf16[2048,4,128]{2,1,0:T(4,128)(2,1)}, u32[]{:S(2)}, u32[]{:S(2)}) async-start(bf16[2048,4,128]{2,1,0:T(4,128)(2,1)} %copy.73), calls=%async_computation | async-start | bytes 4194304 | tf_op jit(solution)/shard_map/all_to_all | solution.py:107
  183.8 49.3 %copy-start.5 = (f32[2,256,768]{2,1,0:T(8,128)S(1)}, f32[2,256,768]{2,1,0:T(8,128)}, u32[]{:S(2)}) copy-start(f32[2,256,768]{2,1,0:T(8,128)} %get-tuple-element.29) | copy-start | bytes 4718596
  183.9 106.9 %all-reduce.3.cloned.1.call-start = ((), (), s32[]{:S(2)}) async-start(), calls=%async_computation.3 | async-start | bytes 2359296 | tf_op jit(solution)/shard_map/psum | solution.py:151
  237.3 173.2 %reduce-scatter.2.cloned.1.call-start = ((), (), s32[]{:S(2)}) async-start(), calls=%async_computation.2 | async-start | bytes 18874368 | tf_op jit(solution)/shard_map/reduce_scatter | solution.py:156
  293.3 117.1 %copy-start.1 = (bf16[768,768]{1,0:T(8,128)(2,1)S(1)}, bf16[768,768]{1,0:T(8,128)(2,1)}, u32[]{:S(2)}) copy-start(bf16[768,768]{1,0:T(8,128)(2,1)} %param.16) | copy-start | bytes 3538948
Sparse Core Ops, SparseCore 0:
  237.4 53.3 all-reduce.2
  294.9 115.4 reduce-scatter.1
